TPU v7x, 32 devices: a whole 2x2x4 slice. The times are simulated.
32 devices in a mesh: group: 4 (over x, core), replica: 8 (over z, y).
Axes of the slice: x: 2, y: 2, z: 4, core: 2. Of those that a mesh axis runs over, the one named last changes fastest.
Arguments:
- grad_parts: bfloat16 [8, 8, 128, 512], P('replica', None, 'group'), may hold values from -1 to 1
- owner_order: int32 [8], replicated, may hold values from 0 to 7, each once
- step_count: int32 [1], replicated, may hold values from 1 to 12
- stat_old: float32 [8, 512, 512], P('replica'), as said below
- root_old: bfloat16 [8, 512, 512], P('replica'), may hold values from -0.25 to 0.25
Outputs:
- update: bfloat16 [8, 128, 512], P(None, 'group')
- stat_new: float32 [8, 512, 512], P('replica')
- root_new: bfloat16 [8, 512, 512], P('replica')
Inputs may be any that keep to these rules, and one draw needn't show every extreme that they name: `stat_old`: each matrix is symmetric positive definite.
All inputs are finite; a program needn't handle non-finite values.
Results may differ from a plain program's by a relative error of at most 0.001.
The roundings to bfloat16 on the way count: a program that leaves them out, or rounds other values in their place, can miss the bound.
Values may be sent and summed in bfloat16 or wider, within the bound.
No kernel may reach another device: no remote copies, remote signals or barrier semaphores. Data moves between devices by JAX's collectives and lax.ppermute only.
A program may use at most 64 MiB of HBM per device.

v0:
```python
import jax
import jax.numpy as jnp
from jax import lax
from jax.sharding import PartitionSpec as P

ITERS = 3
decay_rate = 0.95
epsilon = 0.001


def newton(shifted):
    identity = jnp.eye(shifted.shape[0], dtype=jnp.float32)
    frobenius = jnp.sqrt(jnp.sum(shifted * shifted))
    coupled = shifted / frobenius
    root_iter = identity * frobenius ** (-0.25)
    for repeat in range(ITERS):
        factor = (5.0 * identity - coupled) * 0.25
        root_iter = jnp.dot(root_iter, factor, precision=lax.Precision.HIGHEST)
        if repeat + 1 < ITERS:
            factor_sq = jnp.dot(factor, factor, precision=lax.Precision.HIGHEST)
            factor_quad = jnp.dot(factor_sq, factor_sq, precision=lax.Precision.HIGHEST)
            coupled = jnp.dot(factor_quad, coupled, precision=lax.Precision.HIGHEST)
    return root_iter


def local(grad_parts, owner_order, step_count, stat_old, root_old):
    local_grads = grad_parts[0]
    ordered = local_grads[owner_order]
    received = lax.all_to_all(ordered[None], "replica", split_axis=1, concat_axis=0, tiled=True)
    owned = jnp.sum(received.astype(jnp.float32), axis=0)
    partial_gram = jnp.einsum("bri,brj->bij", owned, owned, precision=lax.Precision.HIGHEST)
    products = jnp.einsum(
        "bri,bij->brj", owned.astype(jnp.bfloat16), root_old, preferred_element_type=jnp.float32
    )
    partial_norm = jnp.sum(products * products, axis=(1, 2))
    gram_matrix, update_norm = lax.psum((partial_gram, partial_norm), "group")
    grad_norm = jnp.trace(gram_matrix, axis1=1, axis2=2)
    graft_scale = jnp.sqrt(grad_norm / (update_norm + 1e-06))
    scaled = (graft_scale[:, None, None] * products).astype(jnp.bfloat16)
    gathered = lax.all_gather(scaled, "replica", axis=0, tiled=True)
    update = jnp.zeros_like(gathered).at[owner_order].set(gathered)
    stat_new = decay_rate * stat_old + (1.0 - decay_rate) * gram_matrix
    correction = 1.0 / (1.0 - decay_rate ** step_count[0].astype(jnp.float32))
    shifted = stat_new * correction + epsilon * jnp.eye(stat_new.shape[1], dtype=jnp.float32)
    root_new = lax.map(newton, shifted).astype(jnp.bfloat16)
    return (update, stat_new, root_new)


def solution(mesh):
    placed = (
        P("replica", None, "group", None),
        P(),
        P(),
        P("replica", None, None),
        P("replica", None, None),
    )
    return jax.shard_map(
        local,
        mesh=mesh,
        in_specs=placed,
        out_specs=(P(None, "group", None), P("replica", None, None), P("replica", None, None)),
        check_vma=False,
    )
```

profile of v0, /device:TPU:0, one launch (start us, length us, event | category | flops | bytes accessed | tf_op | source)
XLA Modules:
  0.0 126.4 jit_solution(15580995075982099753)
XLA Ops:
  7.2 0.0 copy-start
  7.2 0.0 all-reduce.2.cloned.1.call-start
  7.2 0.7 compare_select_fusion
  7.9 1.5 %gather_fusion = bf16[8,32,512]{2,1,0:T(8,128)(2,1)S(1)} fusion(bf16[8,32,512]{2,1,0:T(8,128)(2,1)} %bitcast.40, s32[1024]{0:T(1024)S(1)} %pad_clamp_fusion), kind=kCustom, calls=%fused_computation | custom fusion | bytes 524320 | tf_op jit(solution)/shard_map/gather | solution.py:28
  9.5 16.0 %all_to_all.4 = bf16[1,8,32,512]{3,2,0,1:T(8,128)(2,1)S(1)} all-to-all(bf16[1,8,32,512]{3,2,0,1:T(8,128)(2,1)S(1)} %bitcast.38), channel_id=1, replica_groups=mesh['group'=4,'replica'=8] {'replica'}, dimensions={1} | all-to-all | bytes 524288 | tf_op jit(solution)/shard_map/all_to_all | solution.py:29
  25.5 2.0 %convolution_bitcast_fusion = f32[1,512,512]{2,1,0:T(8,128)} fusion(f32[32,512]{1,0:T(8,128)S(1)} %convert_reduce_fusion), kind=kOutput, calls=%fused_computation.5 | convolution fusion | flops 100663296 | bytes 1114112 | tf_op jit(solution)/shard_map/bri,brj->bij/dot_general | solution.py:31
  27.5 0.0 copy-start.1
  27.5 0.0 all-reduce.2.cloned.1.call-update
  28.4 0.0 copy-done
  28.4 0.8 multiply_reduce_fusion.1
  29.2 6.3 %psum.15 = f32[1]{0:T(128)} all-reduce(f32[1]{0:T(128)} %bitcast.5), channel_id=1, replica_groups=mesh['group'=4,'replica'=8] {'group'}, use_global_device_ids=true, to_apply=%region_4.5 | all-reduce | flops 1 | bytes 8 | tf_op jit(solution)/shard_map/psum | solution.py:36
  36.1 26.8 %all-reduce.2.cloned.1.call-done = f32[1,512,512]{2,1,0:T(8,128)} async-done(((f32[1,512,512]{2,1,0:T(8,128)}), f32[1,512,512]{2,1,0:T(8,128)}) %all-reduce.2.cloned.1.call-update) | async-done | bytes 1048592 | tf_op jit(solution)/shard_map/psum | solution.py:36
  63.0 0.0 copy-done.1
  63.0 2.2 %multiply_reduce_fusion = (f32[]{:T(128)}, f32[1,512,512]{2,1,0:T(8,128)S(1)}, f32[]{:T(128)}) fusion(f32[]{:T(128)} %bitcast.8, f32[1,512,512]{2,1,0:T(8,128)} %all-reduce.2.cloned.1.call-done, f32[1,512,512]{2,1,0:T(8,128)S(1)} %copy-done.1), kind=kLoop, calls=%fused_computation.21 | loop fusion | flops 2883582 | bytes 3145740 | tf_op jit(solution)/shard_map/while/body/eval_jaxpr/reduce_sum | solution.py:13
  65.1 0.0 copy-start.2
  65.8 2.1 %fusion.6 = f32[512,512]{1,0:T(8,128)S(1)} fusion(f32[1,512,512]{2,1,0:T(8,128)S(1)} %get-tuple-element.13, f32[]{:T(128)S(6)} %sqrt.8, f32[]{:T(128)} %bitcast.8), kind=kOutput, calls=%fused_computation.12 | convolution fusion | flops 1612709888 | bytes 2097160 | tf_op jit(solution)/shard_map/while/body/eval_jaxpr/dot_general | solution.py:20
  67.9 0.0 copy-done.2
  67.9 1.8 %fusion.51 = f32[512,512]{1,0:T(8,128)S(1)} fusion(f32[512,512]{1,0:T(8,128)S(1)} %fusion.6), kind=kOutput, calls=%fused_computation.63 | convolution fusion | flops 1610612736 | bytes 2097152 | tf_op jit(solution)/shard_map/while/body/eval_jaxpr/dot_general | solution.py:21
  69.8 3.1 %fusion.8 = f32[512,512]{1,0:T(8,128)S(1)} fusion(f32[512,512]{1,0:T(8,128)S(1)} %fusion.51, f32[1,512,512]{2,1,0:T(8,128)} %copy-done.2, f32[]{:T(128)S(6)} %sqrt.8, f32[]{:T(128)} %bitcast.8), kind=kOutput, calls=%fused_computation.14 | convolution fusion | flops 1611923456 | bytes 3145736 | tf_op jit(solution)/shard_map/while/body/eval_jaxpr/dot_general | solution.py:22
  72.9 1.9 %fusion.16 = f32[512,512]{1,0:T(8,128)S(1)} fusion(f32[512,512]{1,0:T(8,128)S(1)} %fusion.8), kind=kOutput, calls=%fused_computation.28 | convolution fusion | flops 1611661312 | bytes 2097152 | tf_op jit(solution)/shard_map/while/body/eval_jaxpr/dot_general | solution.py:20
  74.9 1.8 %fusion.52 = f32[512,512]{1,0:T(8,128)S(1)} fusion(f32[512,512]{1,0:T(8,128)S(1)} %fusion.16), kind=kOutput, calls=%fused_computation.64 | convolution fusion | flops 1610612736 | bytes 2097152 | tf_op jit(solution)/shard_map/while/body/eval_jaxpr/dot_general | solution.py:21
  76.7 1.9 %fusion = f32[512,512]{1,0:T(8,128)S(1)} fusion(f32[512,512]{1,0:T(8,128)S(1)} %fusion.52, f32[512,512]{1,0:T(8,128)S(1)} %fusion.8), kind=kOutput, calls=%fused_computation.6 | convolution fusion | flops 1611661312 | bytes 3145728 | tf_op jit(solution)/shard_map/while/body/eval_jaxpr/dot_general | solution.py:22
  78.6 3.3 %fusion.3 = f32[512,512]{1,0:T(8,128)S(1)} fusion(f32[]{:T(128)S(6)} %pow.9, f32[1,512,512]{2,1,0:T(8,128)} %copy-done.2, f32[]{:T(128)S(6)} %sqrt.8, f32[]{:T(128)} %bitcast.8), kind=kOutput, calls=%fused_computation.10 | convolution fusion | flops 1613496320 | bytes 2097164 | tf_op jit(solution)/shard_map/while/body/eval_jaxpr/dot_general | solution.py:18
  82.0 1.9 %fusion.18 = f32[512,512]{1,0:T(8,128)S(1)} fusion(f32[512,512]{1,0:T(8,128)S(1)} %fusion.3, f32[512,512]{1,0:T(8,128)S(1)} %fusion.8), kind=kOutput, calls=%fused_computation.29 | convolution fusion | flops 1611661312 | bytes 3145728 | tf_op jit(solution)/shard_map/while/body/eval_jaxpr/dot_general | solution.py:18
  84.6 30.8 %all-gather = bf16[256,512]{1,0:T(8,128)(2,1)S(1)} all-gather(bf16[32,512]{1,0:T(8,128)(2,1)S(1)} %multiply_convert_fusion), channel_id=2, replica_groups=mesh['group'=4,'replica'=8] {'replica'}, dimensions={0}, use_global_device_ids=true | all-gather | bytes 294912 | tf_op jit(solution)/shard_map/all_gather | solution.py:40
  115.5 2.6 %fusion.1 = bf16[1,512,512]{2,1,0:T(8,128)(2,1)} fusion(f32[512,512]{1,0:T(8,128)S(1)} %fusion.18, f32[512,512]{1,0:T(8,128)S(1)} %fusion), kind=kOutput, calls=%fused_computation.8 | convolution fusion | flops 1610874880 | bytes 2621440 | tf_op jit(solution)/shard_map/while/body/eval_jaxpr/dot_general | solution.py:18
  118.1 0.8 scatter_fusion
  118.9 0.0 copy-start.3
  118.9 0.7 copy-done.3
  (4 shorter events, 0.1 us)
Async XLA Ops:
  7.2 21.2 %copy-start = (bf16[1,512,512]{2,1,0:T(8,128)(2,1)S(1)}, bf16[1,512,512]{2,1,0:T(8,128)(2,1)}, u32[]{:S(2)}) copy-start(bf16[1,512,512]{2,1,0:T(8,128)(2,1)} %param.9) | copy-start | bytes 1572868
  7.2 55.8 %all-reduce.2.cloned.1.call-start = ((), (), s32[]{:S(2)}) async-start(), calls=%async_computation.1 | async-start | bytes 2097152 | tf_op jit(solution)/shard_map/psum | solution.py:36
  27.5 35.4 %copy-start.1 = (f32[1,512,512]{2,1,0:T(8,128)S(1)}, f32[1,512,512]{2,1,0:T(8,128)}, u32[]{:S(2)}) copy-start(f32[1,512,512]{2,1,0:T(8,128)} %param.8) | copy-start | bytes 3145732
  65.1 2.8 %copy-start.2 = (f32[1,512,512]{2,1,0:T(8,128)}, f32[1,512,512]{2,1,0:T(8,128)S(1)}, u32[]{:S(2)}) copy-start(f32[1,512,512]{2,1,0:T(8,128)S(1)} %get-tuple-element.13) | copy-start | bytes 3145732
  118.9 0.7 copy-start.3
Sparse Core Ops, SparseCore 0:
  27.7 35.2 all-reduce.1
where the time goes:
time: 127 us; the launch traced here: 126 us
  blocking collectives  53.1 us (42%)
  waiting for transfers between devices  26.9 us (21%)
  matrix products  23.4 us (18%)
  between operations  17.1 us (13%)
  local copies, waits for them, and re-layouts  3 us (2%)
  other arithmetic  2.95 us (2%)
    all_gather x1, blocking collectives, local(): gathered = lax.all_gather(scaled, 'replica', axis=0, tiled=True)  30.8 us
    psum x1, waiting for transfers between devices, local(): gram_matrix, update_norm = lax.psum((partial_gram, partial_norm), 'group')  26.8 us
    all_to_all x1, blocking collectives, local(): lax.all_to_all(ordered[None], 'replica', split_axis=1, concat_axis=0, til...  16 us
    dot_general x3, matrix products, newton(): root_iter = jnp.dot(root_iter, factor, precision=lax.Precision.HIGHEST)  7.9 us
    psum x1, blocking collectives, local(): gram_matrix, update_norm = lax.psum((partial_gram, partial_norm), 'group')  6.27 us
    dot_general x2, matrix products, newton(): coupled = jnp.dot(factor_quad, coupled, precision=lax.Precision.HIGHEST)  5 us
    dot_general x2, matrix products, newton(): factor_sq = jnp.dot(factor, factor, precision=lax.Precision.HIGHEST)  3.98 us
    dot_general x2, matrix products, newton(): factor_quad = jnp.dot(factor_sq, factor_sq, precision=lax.Precision.HIGHEST)  3.68 us
  transfers between devices with their start and end apart: 1, of which 1 were waited for; matrix products, arithmetic and copies ran while one was open for 1% of the time, Pallas kernels for 0%

commit v1 on v0

--- a/solution.py
+++ b/solution.py
@@ -37,7 +37,25 @@
     grad_norm = jnp.trace(gram_matrix, axis1=1, axis2=2)
     graft_scale = jnp.sqrt(grad_norm / (update_norm + 1e-06))
     scaled = (graft_scale[:, None, None] * products).astype(jnp.bfloat16)
-    gathered = lax.all_gather(scaled, "replica", axis=0, tiled=True)
+
+    def post_table(along_axis, tile_in):
+        next_value = lax.axis_size(along_axis)
+        part_now = lax.axis_index(along_axis)
+        work_now, w_next, h_now = (next_value, part_now, tile_in.shape[0])
+        piece_next, heard = (tile_in, 1)
+        while heard < work_now:
+            block_list = []
+            c = 0
+            while c < work_now:
+                block_list.append((c, (c - heard) % work_now))
+                c = c + 1
+            r2 = lax.ppermute(piece_next, axis_name=along_axis, perm=block_list)
+            piece_next = jnp.concatenate([piece_next, r2], axis=0)
+            heard = 2 * heard
+        passed = jnp.roll(piece_next, w_next * h_now, 0)
+        return passed
+
+    gathered = post_table("replica", scaled)
     update = jnp.zeros_like(gathered).at[owner_order].set(gathered)
     stat_new = decay_rate * stat_old + (1.0 - decay_rate) * gram_matrix
     correction = 1.0 / (1.0 - decay_rate ** step_count[0].astype(jnp.float32))

time: 127 us -> 110 us (0.87)
  blocking collectives: 53.1 us -> 22.3 us
  waiting for transfers between devices: 26.9 us -> 34.5 us
  starting transfers between devices: 0.04 us -> 5.68 us
    all_gather x1 -> x0, blocking collectives: 30.8 us -> none  [local(): gathered = lax.all_gather(scaled, 'replica', axis=0, tiled=True)]
    ppermute x0 -> x3, waiting for transfers between devices: none -> 7.66 us  [post_table(): r2 = lax.ppermute(piece_next, axis_name=along_axis, perm=block_list)]
    ppermute x0 -> x3, starting transfers between devices: none -> 5.64 us  [post_table(): r2 = lax.ppermute(piece_next, axis_name=along_axis, perm=block_list)]
  transfers between devices with their start and end apart: 1 -> 4, of which waited for: 1 -> 3; matrix products, arithmetic and copies ran while one was open for 1% -> 5% of each run, Pallas kernels for 0% -> 0%
where the time goes in v1:
time: 110 us; the launch traced here: 109 us
  waiting for transfers between devices  34.5 us (31%)
  matrix products  23.4 us (21%)
  blocking collectives  22.3 us (20%)
  between operations  17.2 us (16%)
  starting transfers between devices  5.68 us (5%)
  local copies, waits for them, and re-layouts  3.07 us (3%)
  other arithmetic  2.98 us (3%)
    psum x1, waiting for transfers between devices, local(): gram_matrix, update_norm = lax.psum((partial_gram, partial_norm), 'group')  26.8 us
    all_to_all x1, blocking collectives, local(): lax.all_to_all(ordered[None], 'replica', split_axis=1, concat_axis=0, til...  16 us
    dot_general x3, matrix products, newton(): root_iter = jnp.dot(root_iter, factor, precision=lax.Precision.HIGHEST)  7.89 us
    ppermute x3, waiting for transfers between devices, post_table(): r2 = lax.ppermute(piece_next, axis_name=along_axis, perm=block_list)  7.66 us
    psum x1, blocking collectives, local(): gram_matrix, update_norm = lax.psum((partial_gram, partial_norm), 'group')  6.27 us
    ppermute x3, starting transfers between devices, post_table(): r2 = lax.ppermute(piece_next, axis_name=along_axis, perm=block_list)  5.64 us
    dot_general x2, matrix products, newton(): coupled = jnp.dot(factor_quad, coupled, precision=lax.Precision.HIGHEST)  5 us
    dot_general x2, matrix products, newton(): factor_sq = jnp.dot(factor, factor, precision=lax.Precision.HIGHEST)  3.98 us
  transfers between devices with their start and end apart: 4, of which 3 were waited for; matrix products, arithmetic and copies ran while one was open for 5% of the time, Pallas kernels for 0%

profile of v1, /device:TPU:0, one launch (start us, length us, event | category | flops | bytes accessed | tf_op | source)
XLA Modules:
  0.0 109.1 jit_solution(11931011163135831642)
XLA Ops:
  7.2 0.0 copy-start
  7.2 0.0 all-reduce.2.cloned.1.call-start
  7.2 0.7 compare_select_fusion
  7.9 1.5 %gather_fusion = bf16[8,32,512]{2,1,0:T(8,128)(2,1)S(1)} fusion(bf16[8,32,512]{2,1,0:T(8,128)(2,1)} %bitcast.41, s32[1024]{0:T(1024)S(1)} %pad_clamp_fusion), kind=kCustom, calls=%fused_computation | custom fusion | bytes 524320 | tf_op jit(solution)/shard_map/gather | solution.py:28
  9.5 16.0 %all_to_all.4 = bf16[1,8,32,512]{3,2,0,1:T(8,128)(2,1)S(1)} all-to-all(bf16[1,8,32,512]{3,2,0,1:T(8,128)(2,1)S(1)} %bitcast.40), channel_id=1, replica_groups=mesh['group'=4,'replica'=8] {'replica'}, dimensions={1} | all-to-all | bytes 524288 | tf_op jit(solution)/shard_map/all_to_all | solution.py:29
  25.5 2.0 %convolution_bitcast_fusion = f32[1,512,512]{2,1,0:T(8,128)} fusion(f32[32,512]{1,0:T(8,128)S(1)} %convert_reduce_fusion), kind=kOutput, calls=%fused_computation.5 | convolution fusion | flops 100663296 | bytes 1114112 | tf_op jit(solution)/shard_map/bri,brj->bij/dot_general | solution.py:31
  27.5 0.0 copy-start.1
  27.5 0.0 all-reduce.2.cloned.1.call-update
  28.4 0.0 copy-done
  28.4 0.8 multiply_reduce_fusion.1
  29.2 6.3 %psum.15 = f32[1]{0:T(128)} all-reduce(f32[1]{0:T(128)} %bitcast.5), channel_id=1, replica_groups=mesh['group'=4,'replica'=8] {'group'}, use_global_device_ids=true, to_apply=%region_4.5 | all-reduce | flops 1 | bytes 8 | tf_op jit(solution)/shard_map/psum | solution.py:36
  36.1 26.8 %all-reduce.2.cloned.1.call-done = f32[1,512,512]{2,1,0:T(8,128)} async-done(((f32[1,512,512]{2,1,0:T(8,128)}), f32[1,512,512]{2,1,0:T(8,128)}) %all-reduce.2.cloned.1.call-update) | async-done | bytes 1048592 | tf_op jit(solution)/shard_map/psum | solution.py:36
  63.0 0.0 copy-done.1
  63.0 2.2 %multiply_reduce_fusion = (f32[]{:T(128)}, f32[1,512,512]{2,1,0:T(8,128)S(1)}, f32[]{:T(128)}) fusion(f32[]{:T(128)} %bitcast.8, f32[1,512,512]{2,1,0:T(8,128)} %all-reduce.2.cloned.1.call-done, f32[1,512,512]{2,1,0:T(8,128)S(1)} %copy-done.1), kind=kLoop, calls=%fused_computation.21 | loop fusion | flops 2883582 | bytes 3145740 | tf_op jit(solution)/shard_map/while/body/eval_jaxpr/reduce_sum | solution.py:13
  65.1 0.0 copy-start.2
  65.8 2.1 %fusion.6 = f32[512,512]{1,0:T(8,128)S(1)} fusion(f32[1,512,512]{2,1,0:T(8,128)S(1)} %get-tuple-element.13, f32[]{:T(128)S(6)} %sqrt.8, f32[]{:T(128)} %bitcast.8), kind=kOutput, calls=%fused_computation.12 | convolution fusion | flops 1612709888 | bytes 2097160 | tf_op jit(solution)/shard_map/while/body/eval_jaxpr/dot_general | solution.py:20
  67.9 0.0 copy-done.2
  67.9 1.8 %fusion.53 = f32[512,512]{1,0:T(8,128)S(1)} fusion(f32[512,512]{1,0:T(8,128)S(1)} %fusion.6), kind=kOutput, calls=%fused_computation.75 | convolution fusion | flops 1610612736 | bytes 2097152 | tf_op jit(solution)/shard_map/while/body/eval_jaxpr/dot_general | solution.py:21
  69.8 3.1 %fusion.8 = f32[512,512]{1,0:T(8,128)S(1)} fusion(f32[512,512]{1,0:T(8,128)S(1)} %fusion.53, f32[1,512,512]{2,1,0:T(8,128)} %copy-done.2, f32[]{:T(128)S(6)} %sqrt.8, f32[]{:T(128)} %bitcast.8), kind=kOutput, calls=%fused_computation.14 | convolution fusion | flops 1611923456 | bytes 3145736 | tf_op jit(solution)/shard_map/while/body/eval_jaxpr/dot_general | solution.py:22
  72.9 1.9 %fusion.16 = f32[512,512]{1,0:T(8,128)S(1)} fusion(f32[512,512]{1,0:T(8,128)S(1)} %fusion.8), kind=kOutput, calls=%fused_computation.28 | convolution fusion | flops 1611661312 | bytes 2097152 | tf_op jit(solution)/shard_map/while/body/eval_jaxpr/dot_general | solution.py:20
  74.9 1.8 %fusion.54 = f32[512,512]{1,0:T(8,128)S(1)} fusion(f32[512,512]{1,0:T(8,128)S(1)} %fusion.16), kind=kOutput, calls=%fused_computation.76 | convolution fusion | flops 1610612736 | bytes 2097152 | tf_op jit(solution)/shard_map/while/body/eval_jaxpr/dot_general | solution.py:21
  76.7 1.9 %fusion = f32[512,512]{1,0:T(8,128)S(1)} fusion(f32[512,512]{1,0:T(8,128)S(1)} %fusion.54, f32[512,512]{1,0:T(8,128)S(1)} %fusion.8), kind=kOutput, calls=%fused_computation.6 | convolution fusion | flops 1611661312 | bytes 3145728 | tf_op jit(solution)/shard_map/while/body/eval_jaxpr/dot_general | solution.py:22
  78.6 3.3 %fusion.3 = f32[512,512]{1,0:T(8,128)S(1)} fusion(f32[]{:T(128)S(6)} %pow.9, f32[1,512,512]{2,1,0:T(8,128)} %copy-done.2, f32[]{:T(128)S(6)} %sqrt.8, f32[]{:T(128)} %bitcast.8), kind=kOutput, calls=%fused_computation.10 | convolution fusion | flops 1613496320 | bytes 2097164 | tf_op jit(solution)/shard_map/while/body/eval_jaxpr/dot_general | solution.py:18
  82.7 4.3 %collective-permute-start = (bf16[1,32,512]{2,1,0:T(8,128)(2,1)S(1)}, bf16[1,32,512]{2,1,0:T(8,128)(2,1)S(1)}, u32[]{:S(2)}, u32[]{:S(2)}) collective-permute-start(bf16[1,32,512]{2,1,0:T(8,128)(2,1)S(1)} %get-tuple-element.15), channel_id=1, source_target_pairs={{0,7},{1,0},{2,1},{3,2},{4,3},{5,4},{6,5},{7,6},{8,15},{9,8},{10,9... | collective-permute-start | bytes 98312 | tf_op jit(solution)/shard_map/ppermute | solution.py:52
  87.0 1.9 %fusion.18 = f32[512,512]{1,0:T(8,128)S(1)} fusion(f32[512,512]{1,0:T(8,128)S(1)} %fusion.3, f32[512,512]{1,0:T(8,128)S(1)} %fusion.8), kind=kOutput, calls=%fused_computation.29 | convolution fusion | flops 1611661312 | bytes 3145728 | tf_op jit(solution)/shard_map/while/body/eval_jaxpr/dot_general | solution.py:18
  88.9 0.0 collective-permute-done
  89.0 1.1 %collective-permute-start.1 = (bf16[2,32,512]{2,1,0:T(8,128)(2,1)S(1)}, bf16[2,32,512]{2,1,0:T(8,128)(2,1)S(1)}, u32[]{:S(2)}, u32[]{:S(2)}) collective-permute-start(bf16[2,32,512]{2,1,0:T(8,128)(2,1)S(1)} %pad_maximum_fusion.1), channel_id=1, source_target_pairs={{0,6},{1,7},{2,0},{3,1},{4,2},{5,3},{6,4},{7,5},{8,14},{9,15},{10,... | collective-permute-start | bytes 196616 | tf_op jit(solution)/shard_map/ppermute | solution.py:52
  90.1 2.6 %fusion.1 = bf16[1,512,512]{2,1,0:T(8,128)(2,1)} fusion(f32[512,512]{1,0:T(8,128)S(1)} %fusion.18, f32[512,512]{1,0:T(8,128)S(1)} %fusion), kind=kOutput, calls=%fused_computation.8 | convolution fusion | flops 1610874880 | bytes 2621440 | tf_op jit(solution)/shard_map/while/body/eval_jaxpr/dot_general | solution.py:18
  92.7 0.6 collective-permute-done.1
  93.3 0.2 collective-permute-start.2
  93.5 7.1 %collective-permute-done.2 = bf16[4,32,512]{2,1,0:T(8,128)(2,1)S(1)} collective-permute-done((bf16[4,32,512]{2,1,0:T(8,128)(2,1)S(1)}, bf16[4,32,512]{2,1,0:T(8,128)(2,1)S(1)}, u32[]{:S(2)}, u32[]{:S(2)}) %collective-permute-start.2) | collective-permute-done | bytes 131104 | tf_op jit(solution)/shard_map/ppermute | solution.py:52
  100.8 0.8 scatter_fusion
  101.5 0.0 copy-start.3
  101.5 0.7 copy-done.3
  (14 shorter events, 0.2 us)
Async XLA Ops:
  7.2 21.2 %copy-start = (bf16[1,512,512]{2,1,0:T(8,128)(2,1)S(1)}, bf16[1,512,512]{2,1,0:T(8,128)(2,1)}, u32[]{:S(2)}) copy-start(bf16[1,512,512]{2,1,0:T(8,128)(2,1)} %param.9) | copy-start | bytes 1572868
  7.2 55.8 %all-reduce.2.cloned.1.call-start = ((), (), s32[]{:S(2)}) async-start(), calls=%async_computation.1 | async-start | bytes 2097152 | tf_op jit(solution)/shard_map/psum | solution.py:36
  27.5 35.4 %copy-start.1 = (f32[1,512,512]{2,1,0:T(8,128)S(1)}, f32[1,512,512]{2,1,0:T(8,128)}, u32[]{:S(2)}) copy-start(f32[1,512,512]{2,1,0:T(8,128)} %param.8) | copy-start | bytes 3145732
  65.1 2.8 %copy-start.2 = (f32[1,512,512]{2,1,0:T(8,128)}, f32[1,512,512]{2,1,0:T(8,128)S(1)}, u32[]{:S(2)}) copy-start(f32[1,512,512]{2,1,0:T(8,128)S(1)} %get-tuple-element.13) | copy-start | bytes 3145732
  82.7 6.2 %collective-permute-start = (bf16[1,32,512]{2,1,0:T(8,128)(2,1)S(1)}, bf16[1,32,512]{2,1,0:T(8,128)(2,1)S(1)}, u32[]{:S(2)}, u32[]{:S(2)}) collective-permute-start(bf16[1,32,512]{2,1,0:T(8,128)(2,1)S(1)} %get-tuple-element.15), channel_id=1, source_target_pairs={{0,7},{1,0},{2,1},{3,2},{4,3},{5,4},{6,5},{7,6},{8,15},{9,8},{10,9... | collective-permute-start | bytes 98312 | tf_op jit(solution)/shard_map/ppermute | solution.py:52
  89.0 4.3 %collective-permute-start.1 = (bf16[2,32,512]{2,1,0:T(8,128)(2,1)S(1)}, bf16[2,32,512]{2,1,0:T(8,128)(2,1)S(1)}, u32[]{:S(2)}, u32[]{:S(2)}) collective-permute-start(bf16[2,32,512]{2,1,0:T(8,128)(2,1)S(1)} %pad_maximum_fusion.1), channel_id=1, source_target_pairs={{0,6},{1,7},{2,0},{3,1},{4,2},{5,3},{6,4},{7,5},{8,14},{9,15},{10,... | collective-permute-start | bytes 196616 | tf_op jit(solution)/shard_map/ppermute | solution.py:52
  93.3 7.3 %collective-permute-start.2 = (bf16[4,32,512]{2,1,0:T(8,128)(2,1)S(1)}, bf16[4,32,512]{2,1,0:T(8,128)(2,1)S(1)}, u32[]{:S(2)}, u32[]{:S(2)}) collective-permute-start(bf16[4,32,512]{2,1,0:T(8,128)(2,1)S(1)} %pad_maximum_fusion), channel_id=1, source_target_pairs={{0,4},{1,5},{2,6},{3,7},{4,0},{5,1},{6,2},{7,3},{8,12},{9,13},{10,... | collective-permute-start | bytes 393224 | tf_op jit(solution)/shard_map/ppermute | solution.py:52
  101.5 0.7 copy-start.3
Sparse Core Ops, SparseCore 0:
  27.7 35.2 all-reduce.1
